TPU v7x, 512 devices: a whole 4x8x8 slice. The times are simulated.
512 devices in a mesh: dp: 128 (over y, z, core), shard: 4 (over x).
Axes of the slice: x: 4, y: 8, z: 8, core: 2. Of those that a mesh axis runs over, the one named last changes fastest.
Arguments:
- acts: bfloat16 [131072, 1792], P('dp', 'shard'), may hold values from -6 to 6
- grad_out: bfloat16 [131072, 3584], P('dp', 'shard'), may hold values from -0.016479492 to 0.016479492
- projector: bfloat16 [1792, 256], P('shard'), may hold values from -6 to 6
- moment: bfloat16 [256, 3584], P(None, 'shard'), may hold values from -4 to 4
- second: bfloat16 [256, 3584], P(None, 'shard'), may hold values from 0.29882812 to 3
Outputs:
- new_projector: bfloat16 [1792, 256], P('shard')
- new_moment: bfloat16 [256, 3584], P(None, 'shard')
- new_second: bfloat16 [256, 3584], P(None, 'shard')
- weight_update: bfloat16 [1792, 3584], P('dp', 'shard')
All inputs are finite; a program needn't handle non-finite values.
Results may differ from a plain program's by a relative error of at most 0.0055.
Values may be sent and summed in bfloat16 or wider, within the bound.
A program may use at most 64 MiB of HBM per device.

v0:
```python
import jax
import jax.numpy as jnp
from jax import lax
from jax.sharding import PartitionSpec as P

D = 1792
RANK = 256


def shards(acts, grad_out, projector, moment, second):
    inv_width = 1.0 / D**0.5
    partial_value = jnp.dot(acts, projector, preferred_element_type=jnp.float32)
    summed = lax.psum(partial_value, "shard")
    proj_acts = (summed * inv_width).astype(jnp.bfloat16)
    local_grad = jnp.einsum("tr,tf->rf", proj_acts, grad_out, preferred_element_type=jnp.float32)
    proj_grad = lax.psum(local_grad, "dp")
    proj_low = proj_grad.astype(jnp.bfloat16)
    score_terms = jnp.einsum("tf,rf->tr", grad_out, proj_low, preferred_element_type=jnp.float32)
    token_scores = lax.psum(score_terms, "shard").astype(jnp.bfloat16)
    local_sub = jnp.einsum("td,tr->dr", acts, token_scores, preferred_element_type=jnp.float32)
    subspace = lax.psum(local_sub, "dp")
    gram_local = jnp.dot(
        subspace.T, subspace, precision=lax.Precision.HIGHEST, preferred_element_type=jnp.float32
    )
    gram_matrix = lax.psum(gram_local, "shard")
    mean_square = jnp.trace(gram_matrix) / (D * RANK) + 1e-06
    cubic = jnp.dot(
        subspace, gram_matrix, precision=lax.Precision.HIGHEST, preferred_element_type=jnp.float32
    )
    new_projector = (
        (1.5 * subspace - 0.5 * cubic / (mean_square * D)) / jnp.sqrt(mean_square)
    ).astype(jnp.bfloat16)
    moment_f = 0.9 * moment.astype(jnp.float32) + 0.1 * proj_grad
    second_f = 0.95 * second.astype(jnp.float32) + 0.05 * proj_grad * proj_grad
    first_fix = 1.0 - 0.9**20
    second_fix = 1.0 - 0.95**20
    direction = (moment_f / first_fix / (jnp.sqrt(second_f / second_fix) + 1e-08)).astype(
        jnp.bfloat16
    )
    row_count = D // lax.axis_size("dp")
    replica = lax.axis_index("dp")
    all_rows = lax.all_gather(projector, "shard", axis=0, tiled=True)
    own_rows = lax.dynamic_slice_in_dim(all_rows, replica * row_count, row_count, 0)
    weight_update = (
        jnp.dot(own_rows, direction, preferred_element_type=jnp.float32) / RANK**0.5
    ).astype(jnp.bfloat16)
    return (
        new_projector,
        moment_f.astype(jnp.bfloat16),
        second_f.astype(jnp.bfloat16),
        weight_update,
    )


def solution(mesh):
    in_specs = (
        P("dp", "shard"),
        P("dp", "shard"),
        P("shard", None),
        P(None, "shard"),
        P(None, "shard"),
    )
    out_specs = (P("shard", None), P(None, "shard"), P(None, "shard"), P("dp", "shard"))
    return jax.shard_map(shards, mesh=mesh, in_specs=in_specs, out_specs=out_specs, check_vma=False)
```

profile of v0, /device:TPU:1, one launch (start us, length us, event | category | flops | bytes accessed | tf_op | source)
XLA Modules:
  0.0 562.0 jit_solution(5339090869765811914)
XLA Ops:
  7.2 0.0 copy-start
  7.2 0.0 all-reduce.6.cloned.1.call-start
  7.2 2.9 fusion.22
  10.1 0.0 all-reduce.6.cloned.1.call-update
  10.1 0.0 copy-start.3
  10.1 0.0 all-reduce.8.cloned.1.call-start
  10.2 60.6 %all-reduce.6.cloned.1.call-done = f32[1024,256]{1,0:T(8,128)} async-done(((f32[1024,256]{1,0:T(8,128)}), f32[1024,256]{1,0:T(8,128)}) %all-reduce.6.cloned.1.call-update) | async-done | bytes 1048592 | tf_op jit(solution)/shard_map/psum | solution.py:13
  70.8 0.0 copy-done
  70.8 2.9 fusion.7
  73.7 0.0 all-reduce.8.cloned.1.call-update
  73.7 0.0 all-reduce.10.cloned.1.call-start
  73.8 0.0 copy-done.3
  73.8 13.1 %all_gather.3 = bf16[1792,256]{1,0:T(8,128)(2,1)} all-gather(bf16[448,256]{1,0:T(8,128)(2,1)S(1)} %copy-done.3), channel_id=1, replica_groups=mesh['dp'=128,'shard'=4] {'shard'}, dimensions={0}, use_global_device_ids=true | all-gather | bytes 1146880 | tf_op jit(solution)/shard_map/all_gather | solution.py:42
  86.9 187.1 %all-reduce.8.cloned.1.call-done = f32[256,896]{1,0:T(8,128)} async-done(((f32[256,896]{1,0:T(8,128)}), f32[256,896]{1,0:T(8,128)}) %all-reduce.8.cloned.1.call-update) | async-done | bytes 917520 | tf_op jit(solution)/shard_map/psum | solution.py:16
  274.0 1.9 convolution_bitcast_fusion
  275.9 27.1 %all-reduce.13 = bf16[1024,256]{0,1:T(8,128)(2,1)S(1)} all-reduce(f32[1024,256]{0,1:T(8,128)S(1)} %convolution_bitcast_fusion), channel_id=1, replica_groups=mesh['dp'=128,'shard'=4] {'shard'}, use_global_device_ids=true, to_apply=%region_2.0 | all-reduce | flops 262144 | bytes 1572864 | tf_op jit(solution)/shard_map/psum | solution.py:19
  303.0 0.0 copy-start.1
  303.0 2.5 convolution_bitcast_fusion.1
  305.4 0.0 all-reduce.10.cloned.1.call-update
  305.5 0.0 all-reduce.12.cloned.1.call-start
  305.5 0.0 copy-done.1
  305.5 2.6 fusion.4
  308.1 192.2 %all-reduce.10.cloned.1.call-done = f32[448,256]{1,0:T(8,128)} async-done(((f32[448,256]{1,0:T(8,128)}), f32[448,256]{1,0:T(8,128)}) %all-reduce.10.cloned.1.call-update) | async-done | bytes 458768 | tf_op jit(solution)/shard_map/psum | solution.py:21
  500.3 2.9 fusion.23
  503.2 0.0 copy-start.2
  503.2 0.0 all-reduce.12.cloned.1.call-update
  503.2 2.4 fusion.10
  505.7 45.3 %all-reduce.12.cloned.1.call-done = f32[256,256]{1,0:T(8,128)} async-done(((f32[256,256]{1,0:T(8,128)}), f32[256,256]{1,0:T(8,128)}) %all-reduce.12.cloned.1.call-update) | async-done | bytes 262160 | tf_op jit(solution)/shard_map/psum | solution.py:25
  551.0 1.6 select_reduce_fusion
  553.3 0.0 copy-done.2
  553.3 2.2 fusion.3
Async XLA Ops:
  7.2 63.6 %copy-start = (bf16[1024,896]{1,0:T(8,128)(2,1)S(1)}, bf16[1024,896]{1,0:T(8,128)(2,1)}, u32[]{:S(2)}) copy-start(bf16[1024,896]{1,0:T(8,128)(2,1)} %param.6) | copy-start | bytes 5505028
  7.2 63.6 %all-reduce.6.cloned.1.call-start = ((), (), s32[]{:S(2)}) async-start(), calls=%async_computation | async-start | bytes 2097152 | tf_op jit(solution)/shard_map/psum | solution.py:13
  10.1 63.7 %copy-start.3 = (bf16[448,256]{1,0:T(8,128)(2,1)S(1)}, bf16[448,256]{1,0:T(8,128)(2,1)}, u32[]{:S(2)}) copy-start(bf16[448,256]{1,0:T(8,128)(2,1)} %param.7) | copy-start | bytes 688132
  10.1 263.8 %all-reduce.8.cloned.1.call-start = ((), (), s32[]{:S(2)}) async-start(), calls=%async_computation.1 | async-start | bytes 1835008 | tf_op jit(solution)/shard_map/psum | solution.py:16
  73.7 426.6 %all-reduce.10.cloned.1.call-start = ((), (), s32[]{:S(2)}) async-start(), calls=%async_computation.2 | async-start | bytes 917504 | tf_op jit(solution)/shard_map/psum | solution.py:21
  303.0 2.6 copy-start.1
  305.5 245.5 %all-reduce.12.cloned.1.call-start = ((), (), s32[]{:S(2)}) async-start(), calls=%async_computation.3 | async-start | bytes 524288 | tf_op jit(solution)/shard_map/psum | solution.py:25
  503.2 50.1 %copy-start.2 = (f32[448,256]{1,0:T(8,128)S(1)}, f32[448,256]{1,0:T(8,128)}, u32[]{:S(2)}) copy-start(f32[448,256]{1,0:T(8,128)} %all-reduce.10.cloned.1.call-done) | copy-start | bytes 1376260
Sparse Core Ops, SparseCore 0:
  10.3 60.3 all-reduce.5
  74.0 199.8 all-reduce.7
  305.6 194.7 all-reduce.9
  503.4 47.6 all-reduce.11
where the time goes:
time: 564 us; the launch traced here: 562 us
  waiting for transfers between devices  485 us (86%)
  blocking collectives  40.2 us (7%)
  matrix products  17.8 us (3%)
  between operations  14.5 us (3%)
    psum x1, waiting for transfers between devices, shards(): subspace = lax.psum(local_sub, 'dp')  192 us
    psum x1, waiting for transfers between devices, shards(): proj_grad = lax.psum(local_grad, 'dp')  187 us
    psum x1, waiting for transfers between devices, shards(): summed = lax.psum(partial_value, 'shard')  60.6 us
    psum x1, waiting for transfers between devices, shards(): gram_matrix = lax.psum(gram_local, 'shard')  45.3 us
    psum x1, blocking collectives, shards(): token_scores = lax.psum(score_terms, 'shard').astype(jnp.bfloat16)  27.1 us
    all_gather x1, blocking collectives, shards(): all_rows = lax.all_gather(projector, 'shard', axis=0, tiled=True)  13.1 us
  transfers between devices with their start and end apart: 4, of which 4 were waited for; matrix products, arithmetic and copies ran while one was open for 1% of the time, Pallas kernels for 0%

commit v1 on v0

v1 whole, which is shorter than its diff:
```python
import functools

import jax
import jax.numpy as jnp
from jax import lax
from jax.experimental import pallas as pl
from jax.experimental.pallas import tpu as pltpu
from jax.sharding import PartitionSpec as P

D = 1792
F = 3584
RANK = 256
NX, NY, NZ = 4, 8, 8
HALF = RANK // 2
STRIP = HALF // NY
MESH = pl.DeviceIdType.MESH
F32 = jnp.float32
BF16 = jnp.bfloat16


def dot_nt(a, b, precision=None):
    return lax.dot_general(
        a, b, (((1,), (1,)), ((), ())), precision=precision, preferred_element_type=F32
    )


def dot_nn(a, b, precision=None):
    return lax.dot_general(
        a, b, (((1,), (0,)), ((), ())), precision=precision, preferred_element_type=F32
    )


def step_kernel(
    acts, grad_hbm, proj, low_out, new_out, rows_out,
    grad, pt, rows, load_sem,
    xs, xr, xg,
    ys, yr, yg,
    l1, c1, h1, s1, r1, q1, g1,
    l2, c2, h2, s2, r2, q2, g2,
    gr, gf,
    xsend, xrecv, dsend, drecv,
):
    dp, x = lax.axis_index("dp"), lax.axis_index("shard")
    core = lax.rem(dp, 2)
    z = lax.rem(lax.div(dp, 2), NZ)
    y = lax.div(dp, 2 * NZ)
    other = 1 - core
    pos1 = y * other + z * core
    pos2 = y * core + z * other

    def on_x(j):
        return (dp, lax.rem(x + j, NX))

    def on_first(j):
        return ((lax.rem(y + j * other, NY) * NZ + lax.rem(z + j * core, NZ)) * 2 + core, x)

    def on_second(j):
        return ((lax.rem(y + j * core, NY) * NZ + lax.rem(z + j * other, NZ)) * 2 + core, x)

    partner = (dp + 1 - 2 * core, x)
    x_order = (2, 1, 3)
    order = (4, 3, 5, 2, 6, 1, 7)
    pending = []

    def send(src, dst, send_sem, recv_sem, device):
        copy = pltpu.make_async_remote_copy(
            src_ref=src, dst_ref=dst, send_sem=send_sem, recv_sem=recv_sem,
            device_id=device, device_id_type=MESH,
        )
        copy.start()
        pending.append(copy)
        return copy

    barrier = pltpu.get_barrier_semaphore()
    peers = [on_x(j) for j in x_order] + [partner]
    peers += [on_first(j) for j in order] + [on_second(j) for j in order]
    for peer in peers:
        pl.semaphore_signal(barrier, inc=1, device_id=peer, device_id_type=MESH)

    load = pltpu.make_async_copy(grad_hbm, grad, load_sem)
    load.start()

    def eye(n, m, shift):
        r = lax.broadcasted_iota(jnp.int32, (n, m), 0)
        c = lax.broadcasted_iota(jnp.int32, (n, m), 1)
        return jnp.where(r + shift == c, 1.0, 0.0)

    own_block = D // NX
    count = D // (NY * NZ * 2)
    pt[...] = dot_nt(eye(RANK, RANK, 0).astype(BF16), proj[...]).astype(BF16)
    first_row = lax.rem(dp, own_block // count) * count
    rows[x] = dot_nn(eye(16, own_block, first_row).astype(BF16), proj[...]).astype(BF16)

    quarter = acts.shape[0] // NX

    def tokens(ref, q):
        return ref[pl.ds(pl.multiple_of(q * quarter, quarter), quarter), :]

    def x_exchange(slot, term, finish, s, r, g, barrier_wait):
        copies = []
        for j in x_order:
            s[j - 1] = term(lax.rem(x + j, NX)).astype(BF16)
            if barrier_wait and not copies:
                pl.semaphore_wait(barrier, len(peers))
            k = slot + j - 1
            copies.append(send(s.at[j - 1], r.at[j - 1], xsend.at[k], xrecv.at[k], on_x(j)))
        total = term(x)
        for copy, j in zip(copies, x_order):
            copy.wait_recv()
        for j in x_order:
            total = total + r[j - 1].astype(F32)
        g[x] = finish(total).astype(BF16)
        gathers = {}
        for j in x_order:
            k = slot + 3 + j - 1
            gathers[j] = send(g.at[x], g.at[x], xsend.at[k], xrecv.at[k], on_x(j))
        return gathers

    def x_contract(g, gathers, other_ref):
        total = dot_nn(g[x], tokens(other_ref, x))
        for j in (1, 3, 2):
            gathers[j].wait_recv()
            q = lax.rem(x + NX - j, NX)
            total = total + dot_nn(g[q], tokens(other_ref, q))
        return total

    def plane_sum(slot, local, l, c, h, s, r, q, g):
        l[0] = local[:HALF]
        l[1] = local[HALF:]
        swap = send(l.at[other], c, dsend.at[slot], drecv.at[slot], partner)
        swap.wait_recv()
        for i in range(NY):
            strip = l[core, i * STRIP:(i + 1) * STRIP, :] + c[i * STRIP:(i + 1) * STRIP, :]
            h[i] = strip
            s[i] = strip.astype(s.dtype)
        copies = []
        for j in order:
            k = slot + j
            copies.append(
                send(s.at[lax.rem(pos1 + j, NY)], r.at[j - 1], dsend.at[k], drecv.at[k], on_first(j))
            )
        for copy in copies:
            copy.wait_recv()
        total = h[pos1]
        for j in range(1, NY):
            total = total + r[j - 1].astype(F32)
        q[pos2] = total.astype(q.dtype)
        copies = []
        for j in order:
            k = slot + 7 + j
            copies.append(send(q.at[pos2], q.at[pos2], dsend.at[k], drecv.at[k], on_second(j)))
        for copy in copies:
            copy.wait_recv()
        total = q[0].astype(F32)
        for j in range(1, NZ):
            total = total + q[j].astype(F32)
        g[core, pos1] = total.astype(g.dtype)
        copies = []
        for j in order:
            k = slot + 14 + j
            copies.append(
                send(g.at[core, pos1], g.at[core, pos1], dsend.at[k], drecv.at[k], on_first(j))
            )
        for copy in copies:
            copy.wait_recv()
        send(g.at[core], g.at[core], dsend.at[slot + 22], drecv.at[slot + 22], partner).wait_recv()
        return g[...].reshape(RANK, local.shape[1])

    inv_width = 1.0 / D**0.5
    gathers = x_exchange(
        0, lambda q: dot_nt(pt[...], tokens(acts, q)), lambda v: v * inv_width, xs, xr, xg, True
    )
    row_copies = []
    for j in x_order:
        k = 12 + j - 1
        row_copies.append(send(rows.at[x], rows.at[x], xsend.at[k], xrecv.at[k], on_x(j)))
    load.wait()
    low = plane_sum(0, x_contract(xg, gathers, grad), l1, c1, h1, s1, r1, q1, g1)
    low_out[...] = low
    gathers = x_exchange(
        6, lambda q: dot_nt(low_out[...], tokens(grad, q)), lambda v: v, ys, yr, yg, False
    )
    for copy in row_copies:
        copy.wait_recv()
    rows_out[...] = rows[...]
    sub = plane_sum(23, x_contract(yg, gathers, acts), l2, c2, h2, s2, r2, q2, g2)

    high = lax.Precision.HIGHEST
    mine = g2[core].reshape(HALF, own_block)
    gr[x] = dot_nt(mine, sub, high)
    copies = []
    for j in x_order:
        k = 15 + j - 1
        copies.append(send(gr.at[x], gr.at[x], xsend.at[k], xrecv.at[k], on_x(j)))
    for copy in copies:
        copy.wait_recv()
    gf[core] = gr[0] + gr[1] + gr[2] + gr[3]
    send(gf.at[core], gf.at[core], dsend.at[46], drecv.at[46], partner).wait_recv()
    gram = gf[...].reshape(RANK, RANK)
    trace = jnp.sum(gram * eye(RANK, RANK, 0), axis=(0, 1), keepdims=True)
    mean_square = trace / (D * RANK) + 1e-06
    cubic = dot_nn(gram, sub, high)
    new = (1.5 * sub - 0.5 * cubic / (mean_square * D)) / jnp.sqrt(mean_square)
    new_out[...] = new.astype(BF16)
    for copy in pending:
        copy.wait_send()


def fused(acts, grad_out, projector):
    tokens, own = acts.shape
    wide = grad_out.shape[1]
    quarter = tokens // NX

    def plane(width, part, gathered):
        return [
            pltpu.VMEM((2, HALF, width), F32),
            pltpu.VMEM((HALF, width), F32),
            pltpu.VMEM((NY, STRIP, width), F32),
            pltpu.VMEM((NY, STRIP, width), BF16),
            pltpu.VMEM((NY - 1, STRIP, width), BF16),
            pltpu.VMEM((NZ, STRIP, width), part),
            pltpu.VMEM((2, NY, STRIP, width), gathered),
        ]

    def cross():
        return [
            pltpu.VMEM((NX - 1, RANK, quarter), BF16),
            pltpu.VMEM((NX - 1, RANK, quarter), BF16),
            pltpu.VMEM((NX, RANK, quarter), BF16),
        ]

    vmem = pl.BlockSpec(memory_space=pltpu.VMEM)
    return pl.pallas_call(
        step_kernel,
        out_shape=(
            jax.ShapeDtypeStruct((RANK, wide), BF16),
            jax.ShapeDtypeStruct((RANK, own), BF16),
            jax.ShapeDtypeStruct((NX, 16, RANK), BF16),
        ),
        in_specs=[vmem, pl.BlockSpec(memory_space=pl.ANY), vmem],
        out_specs=(vmem, vmem, vmem),
        scratch_shapes=[
            pltpu.VMEM((tokens, wide), BF16),
            pltpu.VMEM((RANK, own), BF16),
            pltpu.VMEM((NX, 16, RANK), BF16),
            pltpu.SemaphoreType.DMA,
            *cross(),
            *cross(),
            *plane(wide, BF16, BF16),
            *plane(own, F32, F32),
            pltpu.VMEM((NX, HALF, RANK), F32),
            pltpu.VMEM((2, HALF, RANK), F32),
            pltpu.SemaphoreType.DMA((18,)),
            pltpu.SemaphoreType.DMA((18,)),
            pltpu.SemaphoreType.DMA((47,)),
            pltpu.SemaphoreType.DMA((47,)),
        ],
        compiler_params=pltpu.CompilerParams(
            collective_id=0, has_side_effects=True, vmem_limit_bytes=48 * 1024 * 1024
        ),
    )(acts, grad_out, projector)


def shards(acts, grad_out, projector, moment, second):
    low, new_t, rows = fused(acts, grad_out, projector)
    proj_grad = low.astype(F32)
    moment_f = 0.9 * moment.astype(F32) + 0.1 * proj_grad
    second_f = 0.95 * second.astype(F32) + 0.05 * proj_grad * proj_grad
    first_fix = 1.0 - 0.9**20
    second_fix = 1.0 - 0.95**20
    direction = (moment_f / first_fix / (jnp.sqrt(second_f / second_fix) + 1e-08)).astype(BF16)
    row_count = D // lax.axis_size("dp")
    owner = lax.axis_index("dp") // (D // NX // row_count)
    own_rows = lax.dynamic_index_in_dim(rows, owner, 0, keepdims=False)[:row_count]
    weight_update = (
        jnp.dot(own_rows, direction, preferred_element_type=F32) / RANK**0.5
    ).astype(BF16)
    return new_t.T, moment_f.astype(BF16), second_f.astype(BF16), weight_update


def solution(mesh):
    in_specs = (
        P("dp", "shard"),
        P("dp", "shard"),
        P("shard", None),
        P(None, "shard"),
        P(None, "shard"),
    )
    out_specs = (P("shard", None), P(None, "shard"), P(None, "shard"), P("dp", "shard"))
    return jax.shard_map(shards, mesh=mesh, in_specs=in_specs, out_specs=out_specs, check_vma=False)
```

time: 564 us -> 110 us (0.20)
  waiting for transfers between devices: 485 us -> 0 us
  Pallas kernels: 0 us -> 99.6 us
  blocking collectives: 40.2 us -> 0 us
  matrix products: 17.8 us -> 1.4 us
  between operations: 14.5 us -> 0.67 us
    psum x4 -> x0, waiting for transfers between devices: 485 us -> none  [the longest x1 192 us: shards(): subspace = lax.psum(local_sub, 'dp')]
    pallas_call x0 -> x1, Pallas kernels: none -> 99.6 us  [fused(): pl.pallas_call(step_kernel, out_shape=(jax.ShapeDtypeStruct((RANK, wide),...]
    psum x1 -> x0, blocking collectives: 27.1 us -> none  [shards(): token_scores = lax.psum(score_terms, 'shard').astype(jnp.bfloat16)]
    dot_general x7 -> x1, matrix products: 17.8 us -> 1.4 us  [shards(): jnp.dot(own_rows, direction, preferred_element_type=F32) / RANK ** 0.5]
    all_gather x1 -> x0, blocking collectives: 13.1 us -> none  [shards(): all_rows = lax.all_gather(projector, 'shard', axis=0, tiled=True)]
  transfers between devices with their start and end apart: 4 -> 0, of which waited for: 4 -> 0; matrix products, arithmetic and copies ran while one was open for 1% -> 0% of each run, Pallas kernels for 0% -> 0%
where the time goes in v1:
time: 110 us; the launch traced here: 109 us
  Pallas kernels  99.6 us (91%)
  local copies, waits for them, and re-layouts  5.26 us (5%)
  other arithmetic  2.41 us (2%)
  matrix products  1.4 us (1%)
    pallas_call x1, Pallas kernels, fused(): pl.pallas_call(step_kernel, out_shape=(jax.ShapeDtypeStruct((RANK, wide),...  99.6 us
    unnamed x12, local copies, waits for them, and re-layouts  5.26 us
    convert_element_type x1, other arithmetic, shards(): second_f.astype(BF16)  2.41 us

profile of v1, /device:TPU:1, one launch (start us, length us, event | category | flops | bytes accessed | tf_op | source)
XLA Modules:
  0.0 109.4 jit_solution(5569781981929032658)
XLA Ops:
  0.6 0.0 copy-start
  0.6 1.6 %copy.9.acts = bf16[1024,448]{1,0:T(8,128)(2,1)S(1)} copy(bf16[1024,448]{0,1:T(8,128)(2,1)} %param.5) | data formatting | bytes 1835008 | tf_op args[0]
  2.2 0.2 copy-done
  2.4 0.0 copy-start.2
  2.4 0.9 copy-done.2
  3.3 99.6 %shard_map.84 = (bf16[256,896]{1,0:T(8,128)(2,1)S(1)}, bf16[256,448]{1,0:T(8,128)(2,1)S(1)}, bf16[4,16,256]{2,1,0:T(8,128)(2,1)S(1)}) custom-call(bf16[1024,448]{1,0:T(8,128)(2,1)S(1)} %copy.9.acts, bf16[1024,896]{1,0:T(8,128)(2,1)S(1)} %copy-done, bf16[448,256]{1,0:T(8,128)(2,1)S(1)} %copy-done.2), custom_call_target="tpu_custom_call" | custom-call | tf_op jit(solution)/shard_map/pallas_call | solution.py:233
  103.0 0.0 copy-start.1
  103.0 0.7 copy-done.1
  103.7 0.0 copy-start.3
  103.7 0.0 copy-start.4
  103.7 1.9 %copy.10 = bf16[448,256]{1,0:T(8,128)(2,1)} copy(bf16[448,256]{0,1:T(8,128)(2,1)} %bitcast.4) | data formatting | bytes 458752
  105.6 2.4 %fusion.4 = (bf16[256,896]{1,0:T(8,128)(2,1)}, bf16[256,896]{1,0:T(8,128)(2,1)}) fusion(bf16[256,896]{1,0:T(8,128)(2,1)S(1)} %get-tuple-element.8, bf16[256,896]{1,0:T(8,128)(2,1)} %param.9, bf16[256,896]{1,0:T(8,128)(2,1)} %param.8), kind=kLoop, calls=%fused_computation.8 | loop fusion | flops 2752512 | bytes 2293760 | tf_op jit(solution)/shard_map/convert_element_type | solution.py:278
  108.0 0.0 copy-done.3
  108.0 0.0 copy-done.4
  108.0 1.4 %fusion = bf16[14,896]{1,0:T(8,128)(2,1)} fusion(bf16[256,896]{1,0:T(8,128)(2,1)S(1)} %get-tuple-element.8, bf16[256,896]{1,0:T(8,128)(2,1)S(1)} %copy-done.4, bf16[256,896]{1,0:T(8,128)(2,1)S(1)} %copy-done.3, bf16[4,16,256]{2,1,0:T(8,128)(2,1)S(1)} %get-tuple-element.9, s32[]{:T(128)S(6)} %select_n.10), kind=kOutput, calls=%fused_computation.3 | convolution fusion | flops 9888256 | bytes 1409540 | tf_op jit(solution)/shard_map/dot_general | solution.py:276
Async XLA Ops:
  0.6 1.8 %copy-start = (bf16[1024,896]{1,0:T(8,128)(2,1)S(1)}, bf16[1024,896]{1,0:T(8,128)(2,1)}, u32[]{:S(2)}) copy-start(bf16[1024,896]{1,0:T(8,128)(2,1)} %grad_hbm.1) | copy-start | bytes 5505028
  2.4 0.9 copy-start.2
  103.0 0.7 copy-start.1
  103.7 4.3 %copy-start.3 = (bf16[256,896]{1,0:T(8,128)(2,1)S(1)}, bf16[256,896]{1,0:T(8,128)(2,1)}, u32[]{:S(2)}) copy-start(bf16[256,896]{1,0:T(8,128)(2,1)} %param.9) | copy-start | bytes 1376260
  103.7 4.3 %copy-start.4 = (bf16[256,896]{1,0:T(8,128)(2,1)S(1)}, bf16[256,896]{1,0:T(8,128)(2,1)}, u32[]{:S(2)}) copy-start(bf16[256,896]{1,0:T(8,128)(2,1)} %param.8) | copy-start | bytes 1376260

commit v2 on v1

v2 whole, which is shorter than its diff:
```python
import jax
import jax.numpy as jnp
from jax import lax
from jax.experimental import pallas as pl
from jax.experimental.pallas import tpu as pltpu
from jax.sharding import PartitionSpec as P

D = 1792
F = 3584
RANK = 256
NX, NY, NZ = 4, 8, 8
CHUNKS = 2
CHUNK = RANK // CHUNKS
HALF = CHUNK // 2
STRIP = HALF // NY
MESH = pl.DeviceIdType.MESH
F32 = jnp.float32
BF16 = jnp.bfloat16


def dot_nt(a, b, precision=None):
    return lax.dot_general(
        a, b, (((1,), (1,)), ((), ())), precision=precision, preferred_element_type=F32
    )


def dot_nn(a, b, precision=None):
    return lax.dot_general(
        a, b, (((1,), (0,)), ((), ())), precision=precision, preferred_element_type=F32
    )


def step_kernel(
    acts_hbm, grad_hbm, proj_hbm, moment_hbm, second_hbm,
    low_hbm, new_out, update_out,
    acts, grad, proj, moment, second, pt, rows, low,
    xs, xr, xg, ys, yr, yg,
    l1, c1, h1, s1, r1, q1, g1,
    l2, c2, h2, s2, r2, q2, g2,
    gr, gf,
    load, xsend, xrecv, dsend, drecv,
):
    dp, x = lax.axis_index("dp"), lax.axis_index("shard")
    core = lax.rem(dp, 2)
    z = lax.rem(lax.div(dp, 2), NZ)
    y = lax.div(dp, 2 * NZ)
    other = 1 - core
    pos1 = y * other + z * core
    pos2 = y * core + z * other

    def on_x(j):
        return (dp, lax.rem(x + j, NX))

    def on_first(j):
        return ((lax.rem(y + j * other, NY) * NZ + lax.rem(z + j * core, NZ)) * 2 + core, x)

    def on_second(j):
        return ((lax.rem(y + j * core, NY) * NZ + lax.rem(z + j * other, NZ)) * 2 + core, x)

    partner = (dp + 1 - 2 * core, x)
    x_order = (2, 1, 3)
    order = (4, 3, 5, 2, 6, 1, 7)
    pending = []

    def send(src, dst, send_sem, recv_sem, device):
        copy = pltpu.make_async_remote_copy(
            src_ref=src, dst_ref=dst, send_sem=send_sem, recv_sem=recv_sem,
            device_id=device, device_id_type=MESH,
        )
        copy.start()
        pending.append(copy)
        return copy

    barrier = pltpu.get_barrier_semaphore()
    peers = [on_x(j) for j in x_order] + [partner]
    peers += [on_first(j) for j in order] + [on_second(j) for j in order]
    for peer in peers:
        pl.semaphore_signal(barrier, inc=1, device_id=peer, device_id_type=MESH)

    loads = []
    pairs = ((proj_hbm, proj), (acts_hbm, acts), (grad_hbm, grad), (moment_hbm, moment), (second_hbm, second))
    for i, (source, target) in enumerate(pairs):
        loads.append(pltpu.make_async_copy(source, target, load.at[i]))
        loads[-1].start()

    def eye(n, m, shift):
        r = lax.broadcasted_iota(jnp.int32, (n, m), 0)
        c = lax.broadcasted_iota(jnp.int32, (n, m), 1)
        return jnp.where(r + shift == c, 1.0, 0.0)

    own_block = D // NX
    count = D // (NY * NZ * 2)
    quarter = grad.shape[0] // NX
    loads[0].wait()
    pt[...] = dot_nt(eye(RANK, RANK, 0).astype(BF16), proj[...]).astype(BF16)
    first_row = lax.rem(dp, own_block // count) * count
    rows[x] = dot_nn(eye(16, own_block, first_row).astype(BF16), proj[...]).astype(BF16)
    loads[1].wait()

    def span(q):
        return pl.ds(pl.multiple_of(q * quarter, quarter), quarter)

    done = {}

    def once(name, action):
        if name not in done:
            done[name] = action()

    def x_exchange(slot, term, finish, s, r, g):
        copies = []
        for j in x_order:
            s[j - 1] = term(lax.rem(x + j, NX)).astype(BF16)
            once("barrier", lambda: pl.semaphore_wait(barrier, len(peers)))
            k = slot + j - 1
            copies.append(send(s.at[j - 1], r.at[j - 1], xsend.at[k], xrecv.at[k], on_x(j)))
        total = term(x)
        yield
        for copy, j in zip(copies, x_order):
            copy.wait_recv()
            total = total + r[j - 1].astype(F32)
        g[x] = finish(total).astype(BF16)
        gathers = {}
        for j in x_order:
            k = slot + 3 + j - 1
            gathers[j] = send(g.at[x], g.at[x], xsend.at[k], xrecv.at[k], on_x(j))
        return gathers

    def x_contract(g, gathers, term):
        total = term(g[x], x)
        yield
        for j in (1, 3, 2):
            gathers[j].wait_recv()
            q = lax.rem(x + NX - j, NX)
            total = total + term(g[q], q)
        return total

    def plane_sum(slot, local, l, c, h, s, r, q, g):
        l[0] = local[:HALF]
        l[1] = local[HALF:]
        swap = send(l.at[other], c, dsend.at[slot], drecv.at[slot], partner)
        yield
        swap.wait_recv()
        for i in range(NY):
            strip = l[core, i * STRIP:(i + 1) * STRIP, :] + c[i * STRIP:(i + 1) * STRIP, :]
            h[i] = strip
            s[i] = strip.astype(s.dtype)
        copies = []
        for j in order:
            k = slot + j
            copies.append(
                send(s.at[lax.rem(pos1 + j, NY)], r.at[j - 1], dsend.at[k], drecv.at[k], on_first(j))
            )
        yield
        for copy in copies:
            copy.wait_recv()
        total = h[pos1]
        for j in range(1, NY):
            total = total + r[j - 1].astype(F32)
        q[pos2] = total.astype(q.dtype)
        copies = []
        for j in order:
            k = slot + 7 + j
            copies.append(send(q.at[pos2], q.at[pos2], dsend.at[k], drecv.at[k], on_second(j)))
        yield
        for copy in copies:
            copy.wait_recv()
        total = q[0].astype(F32)
        for j in range(1, NZ):
            total = total + q[j].astype(F32)
        g[core, pos1] = total.astype(g.dtype)
        copies = []
        for j in order:
            k = slot + 14 + j
            copies.append(
                send(g.at[core, pos1], g.at[core, pos1], dsend.at[k], drecv.at[k], on_first(j))
            )
        yield
        for copy in copies:
            copy.wait_recv()
        swap = send(g.at[core], g.at[core], dsend.at[slot + 22], drecv.at[slot + 22], partner)
        yield
        swap.wait_recv()

    inv_width = 1.0 / D**0.5
    row_copies = []
    updates = []

    def send_rows():
        for j in x_order:
            k = 12 * CHUNKS + j - 1
            row_copies.append(send(rows.at[x], rows.at[x], xsend.at[k], xrecv.at[k], on_x(j)))

    def wait_rows():
        for copy in row_copies:
            copy.wait_recv()

    def wait_states():
        loads[3].wait()
        loads[4].wait()

    def chain(i):
        part = slice(i * CHUNK, (i + 1) * CHUNK)
        gathers = yield from x_exchange(
            12 * i, lambda q: dot_nn(pt[part, :], acts[:, span(q)]), lambda v: v * inv_width,
            xs.at[i], xr.at[i], xg.at[i],
        )
        once("rows", send_rows)
        once("grad", loads[2].wait)
        local = yield from x_contract(xg.at[i], gathers, lambda v, q: dot_nn(v, grad[span(q), :]))
        bufs = [b.at[i] for b in (l1, c1, h1, s1, r1, q1, g1)]
        yield from plane_sum(46 * i, local, *bufs)
        low[i] = g1[i].reshape(CHUNK, grad.shape[1])
        store = pltpu.make_async_copy(low.at[i], low_hbm.at[pl.ds(i * CHUNK, CHUNK), :], load.at[5 + i])
        store.start()
        exchange = x_exchange(
            12 * i + 6, lambda q: dot_nt(low[i], grad[span(q), :]), lambda v: v,
            ys.at[i], yr.at[i], yg.at[i],
        )
        next(exchange)
        once("states", wait_states)
        once("wait_rows", wait_rows)
        step = low[i].astype(F32)
        moment_f = 0.9 * moment[part, :].astype(F32) + 0.1 * step
        second_f = 0.95 * second[part, :].astype(F32) + 0.05 * step * step
        first_fix = 1.0 - 0.9**20
        second_fix = 1.0 - 0.95**20
        direction = (moment_f / first_fix / (jnp.sqrt(second_f / second_fix) + 1e-08)).astype(BF16)
        mine = rows[lax.div(dp, own_block // count)]
        updates.append(dot_nn(mine[:, part], direction))
        yield
        gathers = yield from exchange
        local = yield from x_contract(yg.at[i], gathers, lambda v, q: dot_nt(v, acts[:, span(q)]))
        bufs = [b.at[i] for b in (l2, c2, h2, s2, r2, q2, g2)]
        yield from plane_sum(46 * i + 23, local, *bufs)
        store.wait()

    live = [chain(i) for i in range(CHUNKS)]
    while live:
        for one in list(live):
            try:
                next(one)
            except StopIteration:
                live.remove(one)

    high = lax.Precision.HIGHEST
    sub = g2[...].reshape(RANK, own_block)
    mine = g2[core].reshape(CHUNK, own_block)
    gr[x] = dot_nt(mine, sub, high).astype(BF16)
    copies = []
    for j in x_order:
        k = 12 * CHUNKS + 3 + j - 1
        copies.append(send(gr.at[x], gr.at[x], xsend.at[k], xrecv.at[k], on_x(j)))
    update_out[...] = (sum(updates) / RANK**0.5).astype(BF16)
    for copy in copies:
        copy.wait_recv()
    total = gr[0].astype(F32)
    for j in range(1, NX):
        total = total + gr[j].astype(F32)
    gf[core] = total
    k = 46 * CHUNKS
    send(gf.at[core], gf.at[core], dsend.at[k], drecv.at[k], partner).wait_recv()
    gram = gf[...].reshape(RANK, RANK)
    trace = jnp.sum(gram * eye(RANK, RANK, 0), axis=(0, 1), keepdims=True)
    mean_square = trace / (D * RANK) + 1e-06
    cubic = dot_nn(gram, sub, high)
    new = (1.5 * sub - 0.5 * cubic / (mean_square * D)) / jnp.sqrt(mean_square)
    new_out[...] = dot_nt(eye(own_block, own_block, 0).astype(BF16), new.astype(BF16)).astype(BF16)
    for copy in pending:
        copy.wait_send()


def fused(acts, grad_out, projector, moment, second):
    own, tokens = acts.shape
    wide = grad_out.shape[1]
    quarter = tokens // NX

    def plane(width, part, gathered):
        return [
            pltpu.VMEM((CHUNKS, 2, HALF, width), F32),
            pltpu.VMEM((CHUNKS, HALF, width), F32),
            pltpu.VMEM((CHUNKS, NY, STRIP, width), F32),
            pltpu.VMEM((CHUNKS, NY, STRIP, width), BF16),
            pltpu.VMEM((CHUNKS, NY - 1, STRIP, width), BF16),
            pltpu.VMEM((CHUNKS, NZ, STRIP, width), part),
            pltpu.VMEM((CHUNKS, 2, NY, STRIP, width), gathered),
        ]

    def cross():
        return [
            pltpu.VMEM((CHUNKS, NX - 1, CHUNK, quarter), BF16),
            pltpu.VMEM((CHUNKS, NX - 1, CHUNK, quarter), BF16),
            pltpu.VMEM((CHUNKS, NX, CHUNK, quarter), BF16),
        ]

    vmem = pl.BlockSpec(memory_space=pltpu.VMEM)
    anywhere = pl.BlockSpec(memory_space=pl.ANY)
    return pl.pallas_call(
        step_kernel,
        out_shape=(
            jax.ShapeDtypeStruct((RANK, wide), BF16),
            jax.ShapeDtypeStruct((own, RANK), BF16),
            jax.ShapeDtypeStruct((16, wide), BF16),
        ),
        in_specs=[anywhere] * 5,
        out_specs=(anywhere, vmem, vmem),
        scratch_shapes=[
            pltpu.VMEM((own, tokens), BF16),
            pltpu.VMEM((tokens, wide), BF16),
            pltpu.VMEM((own, RANK), BF16),
            pltpu.VMEM((RANK, wide), BF16),
            pltpu.VMEM((RANK, wide), BF16),
            pltpu.VMEM((RANK, own), BF16),
            pltpu.VMEM((NX, 16, RANK), BF16),
            pltpu.VMEM((CHUNKS, CHUNK, wide), BF16),
            *cross(),
            *cross(),
            *plane(wide, BF16, BF16),
            *plane(own, F32, F32),
            pltpu.VMEM((NX, CHUNK, RANK), BF16),
            pltpu.VMEM((2, CHUNK, RANK), F32),
            pltpu.SemaphoreType.DMA((5 + CHUNKS,)),
            pltpu.SemaphoreType.DMA((12 * CHUNKS + 6,)),
            pltpu.SemaphoreType.DMA((12 * CHUNKS + 6,)),
            pltpu.SemaphoreType.DMA((46 * CHUNKS + 1,)),
            pltpu.SemaphoreType.DMA((46 * CHUNKS + 1,)),
        ],
        compiler_params=pltpu.CompilerParams(
            collective_id=0, has_side_effects=True, vmem_limit_bytes=67043328
        ),
    )(acts, grad_out, projector, moment, second)


def shards(acts, grad_out, projector, moment, second):
    low, new_projector, update = fused(acts.T, grad_out, projector, moment, second)
    proj_grad = low.astype(F32)
    moment_f = 0.9 * moment.astype(F32) + 0.1 * proj_grad
    second_f = 0.95 * second.astype(F32) + 0.05 * proj_grad * proj_grad
    row_count = D // lax.axis_size("dp")
    return new_projector, moment_f.astype(BF16), second_f.astype(BF16), update[:row_count]


def solution(mesh):
    in_specs = (
        P("dp", "shard"),
        P("dp", "shard"),
        P("shard", None),
        P(None, "shard"),
        P(None, "shard"),
    )
    out_specs = (P("shard", None), P(None, "shard"), P(None, "shard"), P("dp", "shard"))
    return jax.shard_map(shards, mesh=mesh, in_specs=in_specs, out_specs=out_specs, check_vma=False)
```

time: 110 us -> 95.1 us (0.86)
  Pallas kernels: 99.6 us -> 90.4 us
  local copies, waits for them, and re-layouts: 5.26 us -> 1.31 us
  matrix products: 1.4 us -> 0 us
    pallas_call x1, Pallas kernels: 99.6 us -> 90.4 us  [fused(): pl.pallas_call(step_kernel, out_shape=(jax.ShapeDtypeStruct((RANK, wide),...]
    unnamed x12 -> x6, local copies, waits for them, and re-layouts: 5.26 us -> 1.31 us
    dot_general x1 -> x0, matrix products: 1.4 us -> none  [shards(): jnp.dot(own_rows, direction, preferred_element_type=F32) / RANK ** 0.5]
where the time goes in v2:
time: 95.1 us; the launch traced here: 95 us
  Pallas kernels  90.4 us (95%)
  other arithmetic  2.59 us (3%)
  local copies, waits for them, and re-layouts  1.31 us (1%)
    pallas_call x1, Pallas kernels, fused(): pl.pallas_call(step_kernel, out_shape=(jax.ShapeDtypeStruct((RANK, wide),...  90.4 us
    convert_element_type x1, other arithmetic, shards(): second_f.astype(BF16)  2.59 us

profile of v2, /device:TPU:1, one launch (start us, length us, event | category | flops | bytes accessed | tf_op | source)
XLA Modules:
  0.0 95.0 jit_solution(10805378541318113813)
XLA Ops:
  0.6 90.4 %shard_map.84 = (bf16[256,896]{1,0:T(8,128)(2,1)}, bf16[448,256]{1,0:T(8,128)(2,1)}, bf16[16,896]{1,0:T(8,128)(2,1)}) custom-call(bf16[448,1024]{1,0:T(8,128)(2,1)} %bitcast.2, bf16[1024,896]{1,0:T(8,128)(2,1)} %grad_hbm.1, bf16[448,256]{1,0:T(8,128)(2,1)} %proj_hbm.1, bf16[256,896]{1,0:T(8,128)(2,1)} %moment_hbm.1, bf16[256,896]{1,0:T(8,128)(2,1)} %second_hbm.1), custom_call_target="tpu_custom_call" | custom-call | tf_op jit(solution)/shard_map/pallas_call | solution.py:297
  91.1 0.0 copy-start
  91.1 0.0 copy-start.1
  91.1 2.6 %fusion.3 = (bf16[256,896]{1,0:T(8,128)(2,1)}, bf16[256,896]{1,0:T(8,128)(2,1)}) fusion(bf16[256,896]{1,0:T(8,128)(2,1)} %get-tuple-element.8, bf16[256,896]{1,0:T(8,128)(2,1)} %second_hbm.1, bf16[256,896]{1,0:T(8,128)(2,1)} %moment_hbm.1), kind=kLoop, calls=%fused_computation.5 | loop fusion | flops 2752512 | bytes 2293760 | tf_op jit(solution)/shard_map/convert_element_type | solution.py:339
  93.7 0.0 copy-done
  93.7 0.7 copy.11
  94.4 0.0 copy-done.1
  94.4 0.6 copy.12
Async XLA Ops:
  91.1 2.6 %copy-start = (bf16[448,256]{1,0:T(8,128)(2,1)S(1)}, bf16[448,256]{1,0:T(8,128)(2,1)}, u32[]{:S(2)}) copy-start(bf16[448,256]{1,0:T(8,128)(2,1)} %get-tuple-element.16) | copy-start | bytes 688132
  91.1 3.3 %copy-start.1 = (bf16[16,896]{1,0:T(8,128)(2,1)S(1)}, bf16[16,896]{1,0:T(8,128)(2,1)}, u32[]{:S(2)}) copy-start(bf16[16,896]{1,0:T(8,128)(2,1)} %get-tuple-element.9) | copy-start | bytes 86020

commit v3 on v2

--- a/solution.py
+++ b/solution.py
@@ -35,8 +35,8 @@
     low_hbm, new_out, update_out,
     acts, grad, proj, moment, second, pt, rows, low,
     xs, xr, xg, ys, yr, yg,
-    l1, c1, h1, s1, r1, q1, g1,
-    l2, c2, h2, s2, r2, q2, g2,
+    h1, s1, r1, q1, g1,
+    h2, s2, r2, q2, g2,
     gr, gf,
     load, xsend, xrecv, dsend, drecv,
 ):
@@ -57,6 +57,10 @@
     def on_second(j):
         return ((lax.rem(y + j * core, NY) * NZ + lax.rem(z + j * other, NZ)) * 2 + core, x)
 
+    def on_cross(j, axis):
+        row = lax.rem(y + j * (1 - axis), NY)
+        return ((row * NZ + lax.rem(z + j * axis, NZ)) * 2 + other, x)
+
     partner = (dp + 1 - 2 * core, x)
     x_order = (2, 1, 3)
     order = (4, 3, 5, 2, 6, 1, 7)
@@ -74,6 +78,7 @@
     barrier = pltpu.get_barrier_semaphore()
     peers = [on_x(j) for j in x_order] + [partner]
     peers += [on_first(j) for j in order] + [on_second(j) for j in order]
+    peers += [on_cross(j, axis) for axis in (core, other) for j in order]
     for peer in peers:
         pl.semaphore_signal(barrier, inc=1, device_id=peer, device_id_type=MESH)
 
@@ -134,28 +139,30 @@
             total = total + term(g[q], q)
         return total
 
-    def plane_sum(slot, local, l, c, h, s, r, q, g):
-        l[0] = local[:HALF]
-        l[1] = local[HALF:]
-        swap = send(l.at[other], c, dsend.at[slot], drecv.at[slot], partner)
-        yield
-        swap.wait_recv()
-        for i in range(NY):
-            strip = l[core, i * STRIP:(i + 1) * STRIP, :] + c[i * STRIP:(i + 1) * STRIP, :]
-            h[i] = strip
-            s[i] = strip.astype(s.dtype)
+    def plane_sum(slot, local, h, s, r, q, g):
+        for half in range(2):
+            for i in range(NY):
+                first = half * HALF + i * STRIP
+                strip = local[first:first + STRIP]
+                s[half, i] = strip.astype(BF16)
+                h[half, i] = strip
         copies = []
+        at = y * core + z * other
         for j in order:
             k = slot + j
-            copies.append(
-                send(s.at[lax.rem(pos1 + j, NY)], r.at[j - 1], dsend.at[k], drecv.at[k], on_first(j))
-            )
+            source = s.at[core, lax.rem(pos1 + j, NY)]
+            copies.append(send(source, r.at[j - 1], dsend.at[k], drecv.at[k], on_first(j)))
+            k = slot + 22 + j
+            source = s.at[other, lax.rem(at + j, NY)]
+            copies.append(send(source, r.at[6 + j], dsend.at[k], drecv.at[k], on_cross(j, other)))
+        k = slot
+        copies.append(send(s.at[other, at], r.at[14], dsend.at[k], drecv.at[k], partner))
         yield
         for copy in copies:
             copy.wait_recv()
-        total = h[pos1]
-        for j in range(1, NY):
-            total = total + r[j - 1].astype(F32)
+        total = h[core, pos1]
+        for j in range(15):
+            total = total + r[j].astype(F32)
         q[pos2] = total.astype(q.dtype)
         copies = []
         for j in order:
@@ -207,8 +214,8 @@
         once("rows", send_rows)
         once("grad", loads[2].wait)
         local = yield from x_contract(xg.at[i], gathers, lambda v, q: dot_nn(v, grad[span(q), :]))
-        bufs = [b.at[i] for b in (l1, c1, h1, s1, r1, q1, g1)]
-        yield from plane_sum(46 * i, local, *bufs)
+        bufs = [b.at[i] for b in (h1, s1, r1, q1, g1)]
+        yield from plane_sum(76 * i, local, *bufs)
         low[i] = g1[i].reshape(CHUNK, grad.shape[1])
         store = pltpu.make_async_copy(low.at[i], low_hbm.at[pl.ds(i * CHUNK, CHUNK), :], load.at[5 + i])
         store.start()
@@ -230,8 +237,8 @@
         yield
         gathers = yield from exchange
         local = yield from x_contract(yg.at[i], gathers, lambda v, q: dot_nt(v, acts[:, span(q)]))
-        bufs = [b.at[i] for b in (l2, c2, h2, s2, r2, q2, g2)]
-        yield from plane_sum(46 * i + 23, local, *bufs)
+        bufs = [b.at[i] for b in (h2, s2, r2, q2, g2)]
+        yield from plane_sum(76 * i + 38, local, *bufs)
         store.wait()
 
     live = [chain(i) for i in range(CHUNKS)]
@@ -242,10 +249,10 @@
             except StopIteration:
                 live.remove(one)
 
-    high = lax.Precision.HIGHEST
     sub = g2[...].reshape(RANK, own_block)
-    mine = g2[core].reshape(CHUNK, own_block)
-    gr[x] = dot_nt(mine, sub, high).astype(BF16)
+    low_sub = sub.astype(BF16)
+    mine = g2[core].reshape(CHUNK, own_block).astype(BF16)
+    gr[x] = dot_nt(mine, low_sub).astype(BF16)
     copies = []
     for j in x_order:
         k = 12 * CHUNKS + 3 + j - 1
@@ -257,12 +264,12 @@
     for j in range(1, NX):
         total = total + gr[j].astype(F32)
     gf[core] = total
-    k = 46 * CHUNKS
+    k = 76 * CHUNKS
     send(gf.at[core], gf.at[core], dsend.at[k], drecv.at[k], partner).wait_recv()
     gram = gf[...].reshape(RANK, RANK)
     trace = jnp.sum(gram * eye(RANK, RANK, 0), axis=(0, 1), keepdims=True)
     mean_square = trace / (D * RANK) + 1e-06
-    cubic = dot_nn(gram, sub, high)
+    cubic = dot_nn(gram.astype(BF16), low_sub)
     new = (1.5 * sub - 0.5 * cubic / (mean_square * D)) / jnp.sqrt(mean_square)
     new_out[...] = dot_nt(eye(own_block, own_block, 0).astype(BF16), new.astype(BF16)).astype(BF16)
     for copy in pending:
@@ -276,11 +283,9 @@
 
     def plane(width, part, gathered):
         return [
-            pltpu.VMEM((CHUNKS, 2, HALF, width), F32),
-            pltpu.VMEM((CHUNKS, HALF, width), F32),
-            pltpu.VMEM((CHUNKS, NY, STRIP, width), F32),
-            pltpu.VMEM((CHUNKS, NY, STRIP, width), BF16),
-            pltpu.VMEM((CHUNKS, NY - 1, STRIP, width), BF16),
+            pltpu.VMEM((CHUNKS, 2, NY, STRIP, width), F32),
+            pltpu.VMEM((CHUNKS, 2, NY, STRIP, width), BF16),
+            pltpu.VMEM((CHUNKS, 2 * NY - 1, STRIP, width), BF16),
             pltpu.VMEM((CHUNKS, NZ, STRIP, width), part),
             pltpu.VMEM((CHUNKS, 2, NY, STRIP, width), gathered),
         ]
@@ -321,8 +326,8 @@
             pltpu.SemaphoreType.DMA((5 + CHUNKS,)),
             pltpu.SemaphoreType.DMA((12 * CHUNKS + 6,)),
             pltpu.SemaphoreType.DMA((12 * CHUNKS + 6,)),
-            pltpu.SemaphoreType.DMA((46 * CHUNKS + 1,)),
-            pltpu.SemaphoreType.DMA((46 * CHUNKS + 1,)),
+            pltpu.SemaphoreType.DMA((76 * CHUNKS + 1,)),
+            pltpu.SemaphoreType.DMA((76 * CHUNKS + 1,)),
         ],
         compiler_params=pltpu.CompilerParams(
             collective_id=0, has_side_effects=True, vmem_limit_bytes=67043328

time: 95.1 us -> 92.3 us (0.971)
  Pallas kernels: 90.4 us -> 87.6 us
    pallas_call x1, Pallas kernels: 90.4 us -> 87.6 us  [fused(): pl.pallas_call(step_kernel, out_shape=(jax.ShapeDtypeStruct((RANK, wide),...]
where the time goes in v3:
time: 92.3 us; the launch traced here: 92.1 us
  Pallas kernels  87.6 us (95%)
  other arithmetic  2.59 us (3%)
  local copies, waits for them, and re-layouts  1.31 us (1%)
    pallas_call x1, Pallas kernels, fused(): pl.pallas_call(step_kernel, out_shape=(jax.ShapeDtypeStruct((RANK, wide),...  87.6 us
    convert_element_type x1, other arithmetic, shards(): second_f.astype(BF16)  2.59 us

profile of v3, /device:TPU:1, one launch (start us, length us, event | category | flops | bytes accessed | tf_op | source)
XLA Modules:
  0.0 92.1 jit_solution(10115869598987785150)
XLA Ops:
  0.6 87.6 %shard_map.84 = (bf16[256,896]{1,0:T(8,128)(2,1)}, bf16[448,256]{1,0:T(8,128)(2,1)}, bf16[16,896]{1,0:T(8,128)(2,1)}) custom-call(bf16[448,1024]{1,0:T(8,128)(2,1)} %bitcast.2, bf16[1024,896]{1,0:T(8,128)(2,1)} %grad_hbm.1, bf16[448,256]{1,0:T(8,128)(2,1)} %proj_hbm.1, bf16[256,896]{1,0:T(8,128)(2,1)} %moment_hbm.1, bf16[256,896]{1,0:T(8,128)(2,1)} %second_hbm.1), custom_call_target="tpu_custom_call" | custom-call | tf_op jit(solution)/shard_map/pallas_call | solution.py:302
  88.2 0.0 copy-start
  88.2 0.0 copy-start.1
  88.3 2.6 %fusion.3 = (bf16[256,896]{1,0:T(8,128)(2,1)}, bf16[256,896]{1,0:T(8,128)(2,1)}) fusion(bf16[256,896]{1,0:T(8,128)(2,1)} %get-tuple-element.8, bf16[256,896]{1,0:T(8,128)(2,1)} %second_hbm.1, bf16[256,896]{1,0:T(8,128)(2,1)} %moment_hbm.1), kind=kLoop, calls=%fused_computation.5 | loop fusion | flops 2752512 | bytes 2293760 | tf_op jit(solution)/shard_map/convert_element_type | solution.py:344
  90.8 0.0 copy-done
  90.8 0.7 copy.11
  91.5 0.0 copy-done.1
  91.5 0.6 copy.12
Async XLA Ops:
  88.2 2.6 %copy-start = (bf16[448,256]{1,0:T(8,128)(2,1)S(1)}, bf16[448,256]{1,0:T(8,128)(2,1)}, u32[]{:S(2)}) copy-start(bf16[448,256]{1,0:T(8,128)(2,1)} %get-tuple-element.16) | copy-start | bytes 688132
  88.2 3.3 %copy-start.1 = (bf16[16,896]{1,0:T(8,128)(2,1)S(1)}, bf16[16,896]{1,0:T(8,128)(2,1)}, u32[]{:S(2)}) copy-start(bf16[16,896]{1,0:T(8,128)(2,1)} %get-tuple-element.9) | copy-start | bytes 86020

commit v4 on v3

--- a/solution.py
+++ b/solution.py
@@ -37,7 +37,7 @@
     xs, xr, xg, ys, yr, yg,
     h1, s1, r1, q1, g1,
     h2, s2, r2, q2, g2,
-    gr, gf,
+    er, ef, gr, gf,
     load, xsend, xrecv, dsend, drecv,
 ):
     dp, x = lax.axis_index("dp"), lax.axis_index("shard")
@@ -204,6 +204,17 @@
     def wait_states():
         loads[3].wait()
         loads[4].wait()
+
+    early = []
+
+    def block(i):
+        return g2[i].reshape(CHUNK, own_block).astype(BF16)
+
+    def spread(slot, ref):
+        return [
+            send(ref.at[x], ref.at[x], xsend.at[slot + j - 1], xrecv.at[slot + j - 1], on_x(j))
+            for j in x_order
+        ]
 
     def chain(i):
         part = slice(i * CHUNK, (i + 1) * CHUNK)
@@ -240,6 +251,10 @@
         bufs = [b.at[i] for b in (h2, s2, r2, q2, g2)]
         yield from plane_sum(76 * i + 38, local, *bufs)
         store.wait()
+        if i == 0:
+            strip = g2[0, core].reshape(HALF, own_block).astype(BF16)
+            er[x] = dot_nt(strip, block(0)).astype(BF16)
+            early.extend(spread(24 + 3, er))
 
     live = [chain(i) for i in range(CHUNKS)]
     while live:
@@ -250,28 +265,38 @@
                 live.remove(one)
 
     sub = g2[...].reshape(RANK, own_block)
-    low_sub = sub.astype(BF16)
-    mine = g2[core].reshape(CHUNK, own_block).astype(BF16)
-    gr[x] = dot_nt(mine, low_sub).astype(BF16)
-    copies = []
-    for j in x_order:
-        k = 12 * CHUNKS + 3 + j - 1
-        copies.append(send(gr.at[x], gr.at[x], xsend.at[k], xrecv.at[k], on_x(j)))
+    gr[x] = dot_nt(block(core), block(1)).astype(BF16)
+    copies = spread(24 + 6, gr)
+    turned = sub.T
+    low_turned = turned.astype(BF16)
     update_out[...] = (sum(updates) / RANK**0.5).astype(BF16)
-    for copy in copies:
+    for copy in early + copies:
         copy.wait_recv()
-    total = gr[0].astype(F32)
-    for j in range(1, NX):
-        total = total + gr[j].astype(F32)
-    gf[core] = total
+
+    def gathered(ref):
+        total = ref[0].astype(F32)
+        for j in range(1, NX):
+            total = total + ref[j].astype(F32)
+        return total
+
+    ef[core] = gathered(er)
+    gf[core] = gathered(gr)
     k = 76 * CHUNKS
-    send(gf.at[core], gf.at[core], dsend.at[k], drecv.at[k], partner).wait_recv()
-    gram = gf[...].reshape(RANK, RANK)
+    swaps = [
+        send(ef.at[core], ef.at[core], dsend.at[k], drecv.at[k], partner),
+        send(gf.at[core], gf.at[core], dsend.at[k + 1], drecv.at[k + 1], partner),
+    ]
+    for copy in swaps:
+        copy.wait_recv()
+    cross_gram = gf[0]
+    upper = jnp.concatenate([ef[...].reshape(CHUNK, CHUNK), cross_gram], axis=1)
+    lower = jnp.concatenate([cross_gram.T, gf[1]], axis=1)
+    gram = jnp.concatenate([upper, lower], axis=0)
     trace = jnp.sum(gram * eye(RANK, RANK, 0), axis=(0, 1), keepdims=True)
     mean_square = trace / (D * RANK) + 1e-06
-    cubic = dot_nn(gram.astype(BF16), low_sub)
-    new = (1.5 * sub - 0.5 * cubic / (mean_square * D)) / jnp.sqrt(mean_square)
-    new_out[...] = dot_nt(eye(own_block, own_block, 0).astype(BF16), new.astype(BF16)).astype(BF16)
+    cubic = dot_nn(low_turned, gram.astype(BF16))
+    new = (1.5 * turned - 0.5 * cubic / (mean_square * D)) / jnp.sqrt(mean_square)
+    new_out[...] = new.astype(BF16)
     for copy in pending:
         copy.wait_send()
 
@@ -321,13 +346,15 @@
             *cross(),
             *plane(wide, BF16, BF16),
             *plane(own, F32, F32),
-            pltpu.VMEM((NX, CHUNK, RANK), BF16),
-            pltpu.VMEM((2, CHUNK, RANK), F32),
+            pltpu.VMEM((NX, HALF, CHUNK), BF16),
+            pltpu.VMEM((2, HALF, CHUNK), F32),
+            pltpu.VMEM((NX, CHUNK, CHUNK), BF16),
+            pltpu.VMEM((2, CHUNK, CHUNK), F32),
             pltpu.SemaphoreType.DMA((5 + CHUNKS,)),
-            pltpu.SemaphoreType.DMA((12 * CHUNKS + 6,)),
-            pltpu.SemaphoreType.DMA((12 * CHUNKS + 6,)),
-            pltpu.SemaphoreType.DMA((76 * CHUNKS + 1,)),
-            pltpu.SemaphoreType.DMA((76 * CHUNKS + 1,)),
+            pltpu.SemaphoreType.DMA((12 * CHUNKS + 9,)),
+            pltpu.SemaphoreType.DMA((12 * CHUNKS + 9,)),
+            pltpu.SemaphoreType.DMA((76 * CHUNKS + 2,)),
+            pltpu.SemaphoreType.DMA((76 * CHUNKS + 2,)),
         ],
         compiler_params=pltpu.CompilerParams(
             collective_id=0, has_side_effects=True, vmem_limit_bytes=67043328

time: 92.3 us -> 90.9 us (0.985)
  Pallas kernels: 87.6 us -> 86.2 us
    pallas_call x1, Pallas kernels: 87.6 us -> 86.2 us  [fused(): pl.pallas_call(step_kernel, out_shape=(jax.ShapeDtypeStruct((RANK, wide),...]
where the time goes in v4:
time: 90.9 us; the launch traced here: 90.7 us
  Pallas kernels  86.2 us (95%)
  other arithmetic  2.59 us (3%)
  local copies, waits for them, and re-layouts  1.31 us (1%)
    pallas_call x1, Pallas kernels, fused(): pl.pallas_call(step_kernel, out_shape=(jax.ShapeDtypeStruct((RANK, wide),...  86.2 us
    convert_element_type x1, other arithmetic, shards(): second_f.astype(BF16)  2.59 us

profile of v4, /device:TPU:1, one launch (start us, length us, event | category | flops | bytes accessed | tf_op | source)
XLA Modules:
  0.0 90.7 jit_solution(10548266880614579788)
XLA Ops:
  0.6 86.2 %shard_map.84 = (bf16[256,896]{1,0:T(8,128)(2,1)}, bf16[448,256]{1,0:T(8,128)(2,1)}, bf16[16,896]{1,0:T(8,128)(2,1)}) custom-call(bf16[448,1024]{1,0:T(8,128)(2,1)} %bitcast.2, bf16[1024,896]{1,0:T(8,128)(2,1)} %grad_hbm.1, bf16[448,256]{1,0:T(8,128)(2,1)} %proj_hbm.1, bf16[256,896]{1,0:T(8,128)(2,1)} %moment_hbm.1, bf16[256,896]{1,0:T(8,128)(2,1)} %second_hbm.1), custom_call_target="tpu_custom_call" | custom-call | tf_op jit(solution)/shard_map/pallas_call | solution.py:327
  86.8 0.0 copy-start
  86.8 0.0 copy-start.1
  86.8 2.6 %fusion.3 = (bf16[256,896]{1,0:T(8,128)(2,1)}, bf16[256,896]{1,0:T(8,128)(2,1)}) fusion(bf16[256,896]{1,0:T(8,128)(2,1)} %get-tuple-element.8, bf16[256,896]{1,0:T(8,128)(2,1)} %second_hbm.1, bf16[256,896]{1,0:T(8,128)(2,1)} %moment_hbm.1), kind=kLoop, calls=%fused_computation.5 | loop fusion | flops 2752512 | bytes 2293760 | tf_op jit(solution)/shard_map/convert_element_type | solution.py:371
  89.4 0.0 copy-done
  89.4 0.7 copy.11
  90.1 0.0 copy-done.1
  90.1 0.6 copy.12
Async XLA Ops:
  86.8 2.6 %copy-start = (bf16[448,256]{1,0:T(8,128)(2,1)S(1)}, bf16[448,256]{1,0:T(8,128)(2,1)}, u32[]{:S(2)}) copy-start(bf16[448,256]{1,0:T(8,128)(2,1)} %get-tuple-element.16) | copy-start | bytes 688132
  86.8 3.3 %copy-start.1 = (bf16[16,896]{1,0:T(8,128)(2,1)S(1)}, bf16[16,896]{1,0:T(8,128)(2,1)}, u32[]{:S(2)}) copy-start(bf16[16,896]{1,0:T(8,128)(2,1)} %get-tuple-element.9) | copy-start | bytes 86020
